TPU v7x, 32 devices: a whole 2x2x4 slice. The times are simulated.
32 devices in a mesh: rep: 16 (over z, y, x), shard: 2 (over core).
Axes of the slice: x: 2, y: 2, z: 4, core: 2. Of those that a mesh axis runs over, the one named last changes fastest.
Arguments:
- grad_parts: float32 [16, 2, 2, 1024, 512], P('rep', 'shard'), may hold values from -6 to 6
- weights: bfloat16 [2, 1024, 512], P(None, 'shard'), may hold values from -3 to 3
- stat_left: float32 [2, 1024, 1024], P(None, 'shard'), may hold values from -12 to 332, as said below
- stat_right: float32 [512, 512], replicated, may hold values from -12 to 238.27417, as said below
- basis_left: bfloat16 [2, 1024, 1024], P(None, 'shard'), may hold values from -0.1875 to 0.1875
- basis_right: bfloat16 [512, 512], replicated, may hold values from -0.25 to 0.25
- moment_first: float32 [2, 1024, 512], P(None, 'shard'), may hold values from -2 to 2
- moment_second: float32 [2, 1024, 512], P(None, 'shard'), may hold values from 0.05 to 1
Outputs:
- weights_new: bfloat16 [2, 1024, 512], replicated
- basis_left_new: bfloat16 [2, 1024, 1024], P(None, 'shard')
- basis_right_new: bfloat16 [512, 512], replicated
- moment_first_new: float32 [2, 1024, 512], P(None, 'shard')
- moment_second_new: float32 [2, 1024, 512], P(None, 'shard')
Inputs may be any that keep to these rules, and one draw needn't show every extreme that they name: `stat_left`: each block is a symmetric matrix. `stat_right`: a symmetric matrix.
All inputs are finite; a program needn't handle non-finite values.
Results may differ from a plain program's by a relative error of at most 0.015.
Values may be sent and summed in bfloat16 or wider, within the bound.
A program may use at most 128 MiB of HBM per device.

v0:
```python
import jax
import jax.numpy as jnp
from jax import lax
from jax.sharding import PartitionSpec as P

NS_ITERS = 3
stat_beta = 0.9
moment_decay = 0.9
square_decay = 0.95
learn_rate = 0.1
epsilon = 1e-08
norm_epsilon = 1e-06
schulz_linear = 3.4445
schulz_cubic = -4.775
schulz_quintic = 2.0315


def schulz_whole(matrix):
    current = matrix
    for sweep_index in range(NS_ITERS):
        gram_matrix = lax.optimization_barrier(
            jnp.dot(current, current.T, preferred_element_type=jnp.float32).astype(jnp.bfloat16)
        )
        poly_matrix = (
            schulz_cubic * gram_matrix.astype(jnp.float32)
            + schulz_quintic * jnp.dot(gram_matrix, gram_matrix, preferred_element_type=jnp.float32)
        ).astype(jnp.bfloat16)
        current = (
            schulz_linear * current.astype(jnp.float32)
            + jnp.dot(poly_matrix, current, preferred_element_type=jnp.float32)
        ).astype(jnp.bfloat16)
    return current


def schulz_split(start_rows):
    current = start_rows
    for sweep_index in range(NS_ITERS):
        gathered = lax.all_gather(current, "shard", axis=1, tiled=True)
        gram_rows = lax.optimization_barrier(
            jnp.einsum(
                "bik,bjk->bij", current, gathered, preferred_element_type=jnp.float32
            ).astype(jnp.bfloat16)
        )
        gram_block = lax.all_gather(gram_rows, "shard", axis=1, tiled=True)
        poly_rows = (
            schulz_cubic * gram_rows.astype(jnp.float32)
            + schulz_quintic
            * jnp.einsum("bij,bjk->bik", gram_rows, gram_block, preferred_element_type=jnp.float32)
        ).astype(jnp.bfloat16)
        current = (
            schulz_linear * current.astype(jnp.float32)
            + jnp.einsum("bij,bjk->bik", poly_rows, gathered, preferred_element_type=jnp.float32)
        ).astype(jnp.bfloat16)
    return current


def on_device(
    grad_parts, weights, stat_left, stat_right, basis_left, basis_right, moment_first, moment_second
):
    block_count = weights.shape[0]
    row_count = weights.shape[1]
    width_kv = weights.shape[2]
    rep_count = lax.axis_size("rep")
    shard_pos = lax.axis_index("shard")
    row_start = shard_pos * row_count
    partial_value = grad_parts[0, 0]
    grad_total = lax.psum(partial_value, ("rep", "shard")) / rep_count
    grad_full = grad_total.astype(jnp.bfloat16)
    grad_rows = lax.dynamic_slice_in_dim(grad_full, row_start, row_count, 1)
    left_new = stat_beta * stat_left + (1.0 - stat_beta) * jnp.einsum(
        "bik,bjk->bij", grad_rows, grad_full, preferred_element_type=jnp.float32
    )
    grad_flat = grad_rows.reshape(block_count * row_count, width_kv)
    right_terms = jnp.dot(grad_flat.T, grad_flat, preferred_element_type=jnp.float32)
    right_new = stat_beta * stat_right + (1.0 - stat_beta) * lax.psum(right_terms, "shard")
    basis_all = lax.all_gather(basis_left, "shard", axis=1, tiled=True)
    power_rows = jnp.einsum(
        "bij,bjk->bik", left_new.astype(jnp.bfloat16), basis_all, preferred_element_type=jnp.float32
    )
    local_squares = jnp.sum(power_rows * power_rows, axis=(1, 2))
    block_squares = lax.psum(local_squares, "shard")
    start_rows = (power_rows * lax.rsqrt(block_squares + norm_epsilon)[:, None, None]).astype(
        jnp.bfloat16
    )
    basis_left_new = schulz_split(start_rows)
    right_power = jnp.dot(
        right_new.astype(jnp.bfloat16), basis_right, preferred_element_type=jnp.float32
    )
    right_start = (
        right_power * lax.rsqrt(jnp.sum(right_power * right_power) + norm_epsilon)
    ).astype(jnp.bfloat16)
    basis_right_new = schulz_whole(right_start)
    local_turn = jnp.einsum(
        "bji,bjk->bik", basis_left, grad_rows, preferred_element_type=jnp.float32
    )
    rot_left = lax.psum_scatter(
        local_turn.astype(jnp.bfloat16), "shard", scatter_dimension=1, tiled=True
    ).astype(jnp.float32)
    rot_flat = rot_left.reshape(block_count * row_count, width_kv).astype(jnp.bfloat16)
    rotated = jnp.dot(rot_flat, basis_right, preferred_element_type=jnp.float32).reshape(
        block_count, row_count, width_kv
    )
    moment_new = moment_decay * moment_first + (1.0 - moment_decay) * rotated
    square_new = square_decay * moment_second + (1.0 - square_decay) * rotated * rotated
    direction = moment_new / (jnp.sqrt(square_new) + epsilon)
    direction_flat = direction.reshape(block_count * row_count, width_kv).astype(jnp.bfloat16)
    half_turn = (
        jnp.dot(direction_flat, basis_right.T, preferred_element_type=jnp.float32)
        .astype(jnp.bfloat16)
        .reshape(block_count, row_count, width_kv)
    )
    half_all = lax.all_gather(half_turn, "shard", axis=1, tiled=True)
    update = jnp.einsum("bij,bjk->bik", basis_left, half_all, preferred_element_type=jnp.float32)
    weight_rows_new = (weights.astype(jnp.float32) - learn_rate * update).astype(jnp.bfloat16)
    weights_new = lax.all_gather(weight_rows_new, "shard", axis=1, tiled=True)
    return (weights_new, basis_left_new, basis_right_new, moment_new, square_new)


def solution(mesh):
    placed = (
        P("rep", "shard", None, None, None),
        P(None, "shard", None),
        P(None, "shard", None),
        P(),
        P(None, "shard", None),
        P(),
        P(None, "shard", None),
        P(None, "shard", None),
    )
    return jax.shard_map(
        on_device,
        mesh=mesh,
        in_specs=placed,
        out_specs=(
            P(),
            P(None, "shard", None),
            P(),
            P(None, "shard", None),
            P(None, "shard", None),
        ),
        check_vma=False,
    )
```

profile of v0, /device:TPU:0, one launch (start us, length us, event | category | flops | bytes accessed | tf_op | source)
XLA Modules:
  0.0 368.9 jit_solution(12095255493840172626)
XLA Ops:
  9.4 149.6 %all-reduce.3.cloned.1.call-done = f32[2,1024,512]{2,1,0:T(8,128)} async-done(((f32[2,1024,512]{2,1,0:T(8,128)}), f32[2,1024,512]{2,1,0:T(8,128)}) %all-reduce.3.cloned.1.call-update) | async-done | bytes 4194320 | tf_op jit(solution)/shard_map/psum | solution.py:67
  158.9 2.8 multiply_convert_fusion.1
  161.8 9.8 %multiply_reduce_fusion = (f32[2]{0:T(128)S(1)}, f32[2,512,1024]{2,1,0:T(8,128)}) fusion(bf16[2,1024,1024]{2,1,0:T(8,128)(2,1)} %all-gather.14.cloned.1.call-done, f32[2,512,1024]{2,1,0:T(8,128)} %param.10, bf16[2,1024,512]{2,1,0:T(8,128)(2,1)S(1)} %multiply_convert_fusion.1, s32[]{:T(128)S(6)} %select_n.3), kind=kOutput, calls=%fused_computation.7 | convolution fusion | flops 3227516928 | bytes 15728652 | tf_op jit(solution)/shard_map/bij,bjk->bik/dot_general | solution.py:77
  174.0 4.1 %multiply_convert_fusion = bf16[2,512,1024]{2,1,0:T(8,128)(2,1)} fusion(f32[2,512,1024]{2,1,0:T(8,128)} %get-tuple-element.14, f32[2]{0:T(128)S(1)} %add_rsqrt_fusion), kind=kLoop, calls=%fused_computation.6 | loop fusion | flops 2097152 | bytes 6291464 | tf_op jit(solution)/shard_map/convert_element_type | solution.py:82
  178.3 12.5 %all-gather.16.cloned.1.call-done = bf16[2,1024,1024]{2,1,0:T(8,128)(2,1)} async-done(((bf16[2,512,1024]{2,1,0:T(8,128)(2,1)}), bf16[2,1024,1024]{2,1,0:T(8,128)(2,1)}) %all-gather.16.cloned.1.call-update) | async-done | bytes 4194320 | tf_op jit(solution)/shard_map/all_gather | solution.py:38
  190.8 6.5 %convolution_convert_fusion.2 = bf16[2,512,1024]{2,1,0:T(8,128)(2,1)} fusion(bf16[2,512,1024]{2,1,0:T(8,128)(2,1)} %multiply_convert_fusion, bf16[2,1024,1024]{2,1,0:T(8,128)(2,1)} %all-gather.16.cloned.1.call-done), kind=kOutput, calls=%fused_computation.19 | convolution fusion | flops 2148532224 | bytes 8388608 | tf_op jit(solution)/shard_map/bik,bjk->bij/dot_general | solution.py:40
  197.4 14.8 %all-gather.18.cloned.1.call-done = bf16[2,1024,1024]{2,1,0:T(8,128)(2,1)} async-done(((bf16[2,512,1024]{2,1,0:T(8,128)(2,1)}), bf16[2,1024,1024]{2,1,0:T(8,128)(2,1)}) %all-gather.18.cloned.1.call-update) | async-done | bytes 4194320 | tf_op jit(solution)/shard_map/all_gather | solution.py:44
  212.2 10.7 %add_convert_fusion.4 = bf16[2,512,1024]{2,1,0:T(8,128)(2,1)} fusion(bf16[2,512,1024]{2,1,0:T(8,128)(2,1)S(1)} %copy-done.1, bf16[2,1024,1024]{2,1,0:T(8,128)(2,1)} %all-gather.16.cloned.1.call-done, bf16[2,512,1024]{2,1,0:T(8,128)(2,1)} %convolution_convert_fusion.2, bf16[2,1024,1024]{2,1,0:T(8,128)(2,1)} %all-gather.18.cloned.1.call-done), kind=kOutput, calls=%fused_computation.4 | convolution fusion | flops 4304404480 | bytes 14680064 | tf_op jit(solution)/shard_map/bij,bjk->bik/dot_general | solution.py:52
  223.0 4.7 %convert_bitcast_fusion = bf16[2,1024,512]{2,1,0:T(8,128)(2,1)} fusion(bf16[2,512,1024]{2,1,0:T(8,128)(2,1)} %param.12, bf16[2,1024,512]{2,1,0:T(8,128)(2,1)} %copy-done.2, s32[]{:T(128)S(6)} %select_n.3), kind=kOutput, calls=%fused_computation.16 | convolution fusion | flops 1074790400 | bytes 5242884 | tf_op jit(solution)/shard_map/bji,bjk->bik/dot_general | solution.py:93
  227.9 9.9 %all-gather.20.cloned.1.call-done = bf16[2,1024,1024]{2,1,0:T(8,128)(2,1)} async-done(((bf16[2,512,1024]{2,1,0:T(8,128)(2,1)}), bf16[2,1024,1024]{2,1,0:T(8,128)(2,1)}) %all-gather.20.cloned.1.call-update) | async-done | bytes 4194320 | tf_op jit(solution)/shard_map/all_gather | solution.py:38
  237.8 5.9 %convolution_convert_fusion.1 = bf16[2,512,1024]{2,1,0:T(8,128)(2,1)} fusion(bf16[2,512,1024]{2,1,0:T(8,128)(2,1)S(1)} %copy-done.6, bf16[2,1024,1024]{2,1,0:T(8,128)(2,1)} %all-gather.20.cloned.1.call-done), kind=kOutput, calls=%fused_computation.18 | convolution fusion | flops 2148532224 | bytes 8388608 | tf_op jit(solution)/shard_map/bik,bjk->bij/dot_general | solution.py:40
  243.7 7.7 %reduce-scatter.2.cloned.1.call-done = bf16[2,512,512]{2,1,0:T(8,128)(2,1)} async-done(((bf16[2,1024,512]{2,1,0:T(8,128)(2,1)}), bf16[2,512,512]{2,1,0:T(8,128)(2,1)}) %reduce-scatter.2.cloned.1.call-update) | async-done | bytes 1048592 | tf_op jit(solution)/shard_map/reduce_scatter | solution.py:96
  251.4 6.2 %divide_convert_fusion = (bf16[2,512,512]{2,1,0:T(8,128)(2,1)S(1)}, f32[2,512,512]{2,1,0:T(8,128)}, f32[2,512,512]{2,1,0:T(8,128)}) fusion(f32[2,512,512]{2,1,0:T(8,128)} %param.15, f32[2,512,512]{2,1,0:T(8,128)} %param.14, bf16[2,512,512]{2,1,0:T(8,128)(2,1)} %reduce-scatter.2.cloned.1.call-done, bf16[512,512]{1,0:T(8,128)(2,1)S(1)} %copy-done), kind=kOutput, calls=%fused_computation.14 | convolution fusion | flops 542113792 | bytes 11010048 | tf_op jit(solution)/shard_map/dot_general | solution.py:100
  259.7 8.1 %all-gather.22.cloned.1.call-done = bf16[2,1024,1024]{2,1,0:T(8,128)(2,1)} async-done(((bf16[2,512,1024]{2,1,0:T(8,128)(2,1)}), bf16[2,1024,1024]{2,1,0:T(8,128)(2,1)}) %all-gather.22.cloned.1.call-update) | async-done | bytes 4194320 | tf_op jit(solution)/shard_map/all_gather | solution.py:44
  267.8 11.3 %add_convert_fusion.2 = bf16[2,512,1024]{2,1,0:T(8,128)(2,1)} fusion(bf16[2,512,1024]{2,1,0:T(8,128)(2,1)} %add_convert_fusion.4, bf16[2,1024,1024]{2,1,0:T(8,128)(2,1)} %all-gather.20.cloned.1.call-done, bf16[2,512,1024]{2,1,0:T(8,128)(2,1)} %convolution_convert_fusion.1, bf16[2,1024,1024]{2,1,0:T(8,128)(2,1)} %all-gather.22.cloned.1.call-done), kind=kOutput, calls=%fused_computation.2 | convolution fusion | flops 4304404480 | bytes 14680064 | tf_op jit(solution)/shard_map/bij,bjk->bik/dot_general | solution.py:52
  283.3 4.9 %fusion.1 = bf16[2,512,512]{1,2,0:T(8,128)(2,1)} fusion(bf16[2,512,512]{1,2,0:T(8,128)(2,1)} %copy.13, bf16[2,1024,512]{1,2,0:T(8,128)(2,1)} %all-gather.10.cloned.1.call-done, bf16[2,512,1024]{2,1,0:T(8,128)(2,1)} %param.12), kind=kOutput, calls=%fused_computation.13 | convolution fusion | flops 1075838976 | bytes 6291456 | tf_op jit(solution)/shard_map/bij,bjk->bik/dot_general | solution.py:113
  288.4 9.4 %all-gather.24.cloned.1.call-done = bf16[2,1024,1024]{2,1,0:T(8,128)(2,1)} async-done(((bf16[2,512,1024]{2,1,0:T(8,128)(2,1)}), bf16[2,1024,1024]{2,1,0:T(8,128)(2,1)}) %all-gather.24.cloned.1.call-update) | async-done | bytes 4194320 | tf_op jit(solution)/shard_map/all_gather | solution.py:38
  297.8 5.9 %convolution_convert_fusion = bf16[2,512,1024]{2,1,0:T(8,128)(2,1)} fusion(bf16[2,512,1024]{2,1,0:T(8,128)(2,1)S(1)} %copy-done.4, bf16[2,1024,1024]{2,1,0:T(8,128)(2,1)} %all-gather.24.cloned.1.call-done), kind=kOutput, calls=%fused_computation.17 | convolution fusion | flops 2148532224 | bytes 8388608 | tf_op jit(solution)/shard_map/bik,bjk->bij/dot_general | solution.py:40
  303.8 16.8 %all-reduce.5.cloned.1.call-done = f32[512,512]{1,0:T(8,128)} async-done(((f32[512,512]{1,0:T(8,128)}), f32[512,512]{1,0:T(8,128)}) %all-reduce.5.cloned.1.call-update) | async-done | bytes 1048592 | tf_op jit(solution)/shard_map/psum | solution.py:75
  327.7 3.1 fusion.10
  330.8 3.6 all-gather.12.cloned.1.call-done
  334.4 3.9 %copy.15 = bf16[2,1024,512]{2,1,0:T(8,128)(2,1)} copy(bf16[2,1024,512]{1,2,0:T(8,128)(2,1)} %all-gather.12.cloned.1.call-done) | data formatting | bytes 4194304
  338.4 12.3 %all-gather.26.cloned.1.call-done = bf16[2,1024,1024]{2,1,0:T(8,128)(2,1)} async-done(((bf16[2,512,1024]{2,1,0:T(8,128)(2,1)}), bf16[2,1024,1024]{2,1,0:T(8,128)(2,1)}) %all-gather.26.cloned.1.call-update) | async-done | bytes 4194320 | tf_op jit(solution)/shard_map/all_gather | solution.py:44
  350.6 10.7 %add_convert_fusion = bf16[2,512,1024]{2,1,0:T(8,128)(2,1)} fusion(bf16[2,512,1024]{2,1,0:T(8,128)(2,1)S(1)} %copy-done.5, bf16[2,1024,1024]{2,1,0:T(8,128)(2,1)} %all-gather.24.cloned.1.call-done, bf16[2,512,1024]{2,1,0:T(8,128)(2,1)} %convolution_convert_fusion, bf16[2,1024,1024]{2,1,0:T(8,128)(2,1)} %all-gather.26.cloned.1.call-done), kind=kOutput, calls=%fused_computation | convolution fusion | flops 4304404480 | bytes 14680064 | tf_op jit(solution)/shard_map/bij,bjk->bik/dot_general | solution.py:52
  (52 shorter events, 17.3 us)
Async XLA Ops:
  8.0 243.4 %copy-start = (bf16[512,512]{1,0:T(8,128)(2,1)S(1)}, bf16[512,512]{1,0:T(8,128)(2,1)}, u32[]{:S(2)}) copy-start(bf16[512,512]{1,0:T(8,128)(2,1)} %param.13) | copy-start | bytes 1572868
  8.0 150.9 %all-reduce.3.cloned.1.call-start = ((), (), s32[]{:S(2)}) async-start(), calls=%async_computation.1 | async-start | bytes 8388608 | tf_op jit(solution)/shard_map/psum | solution.py:67
  8.7 153.0 %all-gather.14.cloned.1.call-start = ((), (), s32[]{:S(2)}) async-start(), calls=%async_computation.5 | async-start | bytes 6291456 | tf_op jit(solution)/shard_map/all_gather | solution.py:76
  9.3 181.4 %all-gather.16.cloned.1.call-start = ((), (), s32[]{:S(2)}) async-start(), calls=%async_computation.6 | async-start | bytes 6291456 | tf_op jit(solution)/shard_map/all_gather | solution.py:38
  161.7 9.9 %copy-start.2 = (bf16[2,1024,512]{2,1,0:T(8,128)(2,1)}, bf16[2,1024,512]{2,1,0:T(8,128)(2,1)S(1)}, u32[]{:S(2)}) copy-start(bf16[2,1024,512]{2,1,0:T(8,128)(2,1)S(1)} %multiply_convert_fusion.1) | copy-start | bytes 6291460
  178.2 34.0 %copy-start.1 = (bf16[2,512,1024]{2,1,0:T(8,128)(2,1)S(1)}, bf16[2,512,1024]{2,1,0:T(8,128)(2,1)}, u32[]{:S(2)}) copy-start(bf16[2,512,1024]{2,1,0:T(8,128)(2,1)} %multiply_convert_fusion) | copy-start | bytes 6291460
  178.2 33.9 %all-gather.18.cloned.1.call-start = ((), (), s32[]{:S(2)}) async-start(), calls=%async_computation.7 | async-start | bytes 6291456 | tf_op jit(solution)/shard_map/all_gather | solution.py:44
  197.3 40.5 %all-gather.20.cloned.1.call-start = ((), (), s32[]{:S(2)}) async-start(), calls=%async_computation.8 | async-start | bytes 6291456 | tf_op jit(solution)/shard_map/all_gather | solution.py:38
  222.9 14.9 %copy-start.6 = (bf16[2,512,1024]{2,1,0:T(8,128)(2,1)S(1)}, bf16[2,512,1024]{2,1,0:T(8,128)(2,1)}, u32[]{:S(2)}) copy-start(bf16[2,512,1024]{2,1,0:T(8,128)(2,1)} %add_convert_fusion.4) | copy-start | bytes 6291460
  222.9 28.5 %reduce-scatter.2.cloned.1.call-start = ((), (), s32[]{:S(2)}) async-start(), calls=%async_computation.2 | async-start | bytes 3145728 | tf_op jit(solution)/shard_map/reduce_scatter | solution.py:96
  227.7 40.1 %all-gather.22.cloned.1.call-start = ((), (), s32[]{:S(2)}) async-start(), calls=%async_computation.9 | async-start | bytes 6291456 | tf_op jit(solution)/shard_map/all_gather | solution.py:44
  243.7 39.6 %all-gather.10.cloned.1.call-start = ((), (), s32[]{:S(2)}) async-start(), calls=%async_computation.3 | async-start | bytes 3145728 | tf_op jit(solution)/shard_map/all_gather | solution.py:112
  259.6 19.5 %copy-start.3 = (bf16[2,1024,512]{2,1,0:T(8,128)(2,1)S(1)}, bf16[2,1024,512]{2,1,0:T(8,128)(2,1)}, u32[]{:S(2)}) copy-start(bf16[2,1024,512]{2,1,0:T(8,128)(2,1)} %copy-done.2) | copy-start | bytes 6291460
  259.6 38.2 %all-gather.24.cloned.1.call-start = ((), (), s32[]{:S(2)}) async-start(), calls=%async_computation.10 | async-start | bytes 6291456 | tf_op jit(solution)/shard_map/all_gather | solution.py:38
  279.1 41.5 %all-reduce.5.cloned.1.call-start = ((), (), s32[]{:S(2)}) async-start(), calls=%async_computation.12 | async-start | bytes 2097152 | tf_op jit(solution)/shard_map/psum | solution.py:75
  280.9 53.5 %all-gather.12.cloned.1.call-start = ((), (), s32[]{:S(2)}) async-start(), calls=%async_computation.4 | async-start | bytes 3145728 | tf_op jit(solution)/shard_map/all_gather | solution.py:115
  283.2 14.6 %copy-start.4 = (bf16[2,512,1024]{2,1,0:T(8,128)(2,1)S(1)}, bf16[2,512,1024]{2,1,0:T(8,128)(2,1)}, u32[]{:S(2)}) copy-start(bf16[2,512,1024]{2,1,0:T(8,128)(2,1)} %add_convert_fusion.2) | copy-start | bytes 6291460
  288.2 62.5 %all-gather.26.cloned.1.call-start = ((), (), s32[]{:S(2)}) async-start(), calls=%async_computation.11 | async-start | bytes 6291456 | tf_op jit(solution)/shard_map/all_gather | solution.py:44
  327.7 22.9 %copy-start.5 = (bf16[2,512,1024]{2,1,0:T(8,128)(2,1)S(1)}, bf16[2,512,1024]{2,1,0:T(8,128)(2,1)}, u32[]{:S(2)}) copy-start(bf16[2,512,1024]{2,1,0:T(8,128)(2,1)} %add_convert_fusion.2) | copy-start | bytes 6291460
Sparse Core Ops, SparseCore 0:
  14.4 144.5 all-reduce.2
Sparse Core Ops, SparseCore 1:
  10.8 16.3 all-gather.13
  178.3 12.4 all-gather.15
  197.4 14.7 all-gather.17
  223.0 14.7 all-gather.19
  240.6 10.7 reduce-scatter.1
  253.0 14.7 all-gather.21
  269.8 11.6 all-gather.9
  283.0 14.7 all-gather.23
  300.1 20.4 all-reduce.4
  322.7 11.6 all-gather.11
  335.9 14.7 all-gather.25
where the time goes:
time: 369 us
  waiting for transfers between devices  246 us (67%)
  matrix products  88.6 us (24%)
  between operations  16.6 us (4%)
  local copies, waits for them, and re-layouts  7.58 us (2%)
  other arithmetic  6.91 us (2%)
    psum x1, waiting for transfers between devices, on_device(): grad_total = lax.psum(partial_value, ('rep', 'shard')) / rep_count  150 us
    all_gather x3, waiting for transfers between devices, schulz_split(): gram_block = lax.all_gather(gram_rows, 'shard', axis=1, tiled=True)  35.2 us
    dot_general x3, matrix products, schulz_split(): jnp.einsum('bij,bjk->bik', poly_rows, gathered, preferred_element_type=jn...  32.7 us
    all_gather x3, waiting for transfers between devices, schulz_split(): gathered = lax.all_gather(current, 'shard', axis=1, tiled=True)  31.7 us
    dot_general x3, matrix products, schulz_split(): jnp.einsum('bik,bjk->bij', current, gathered, preferred_element_type=jnp....  18.3 us
    psum x1, waiting for transfers between devices, on_device(): lax.psum(right_terms, 'shard')  16.8 us
    dot_general x1, matrix products, on_device(): jnp.einsum('bij,bjk->bik', left_new.astype(jnp.bfloat16), basis_all, pref...  9.84 us
    reduce_scatter x1, waiting for transfers between devices, on_device(): lax.psum_scatter(local_turn.astype(jnp.bfloat16), 'shard', scatter_dimens...  7.67 us
  transfers between devices with their start and end apart: 12, of which 10 were waited for; matrix products, arithmetic and copies ran while one was open for 17% of the time, Pallas kernels for 0%

commit v1 on v0

--- a/solution.py
+++ b/solution.py
@@ -13,6 +13,10 @@
 schulz_linear = 3.4445
 schulz_cubic = -4.775
 schulz_quintic = 2.0315
+
+
+def take_units(incoming_x, shard_axis, mesh_name="rep"):
+    return lax.psum(lax.psum(incoming_x, shard_axis), mesh_name)
 
 
 def schulz_whole(matrix):
@@ -64,7 +68,7 @@
     shard_pos = lax.axis_index("shard")
     row_start = shard_pos * row_count
     partial_value = grad_parts[0, 0]
-    grad_total = lax.psum(partial_value, ("rep", "shard")) / rep_count
+    grad_total = take_units(partial_value, "shard") / rep_count
     grad_full = grad_total.astype(jnp.bfloat16)
     grad_rows = lax.dynamic_slice_in_dim(grad_full, row_start, row_count, 1)
     left_new = stat_beta * stat_left + (1.0 - stat_beta) * jnp.einsum(

time: 369 us -> 441 us (1.20)
  waiting for transfers between devices: 246 us -> 321 us
    psum x1 -> x2, waiting for transfers between devices: 150 us -> 209 us  [take_units(): return lax.psum(lax.psum(incoming_x, shard_axis), mesh_name)]
    all_gather x1, waiting for transfers between devices: 0.03 us -> 11.4 us  [on_device(): basis_all = lax.all_gather(basis_left, 'shard', axis=1, tiled=True)]
  transfers between devices with their start and end apart: 12 -> 13, of which waited for: 10 -> 12; matrix products, arithmetic and copies ran while one was open for 17% -> 14% of each run, Pallas kernels for 0% -> 0%
where the time goes in v1:
time: 441 us
  waiting for transfers between devices  321 us (73%)
  matrix products  87.9 us (20%)
  between operations  14.7 us (3%)
  local copies, waits for them, and re-layouts  7.58 us (2%)
  other arithmetic  6.91 us (2%)
    psum x2, waiting for transfers between devices, take_units(): return lax.psum(lax.psum(incoming_x, shard_axis), mesh_name)  209 us
    all_gather x3, waiting for transfers between devices, schulz_split(): gram_block = lax.all_gather(gram_rows, 'shard', axis=1, tiled=True)  35.6 us
    all_gather x3, waiting for transfers between devices, schulz_split(): gathered = lax.all_gather(current, 'shard', axis=1, tiled=True)  34.6 us
    dot_general x3, matrix products, schulz_split(): jnp.einsum('bij,bjk->bik', poly_rows, gathered, preferred_element_type=jn...  32.7 us
    dot_general x3, matrix products, schulz_split(): jnp.einsum('bik,bjk->bij', current, gathered, preferred_element_type=jnp....  18.3 us
    psum x1, waiting for transfers between devices, on_device(): lax.psum(right_terms, 'shard')  17.3 us
    all_gather x1, waiting for transfers between devices, on_device(): basis_all = lax.all_gather(basis_left, 'shard', axis=1, tiled=True)  11.4 us
    dot_general x1, matrix products, on_device(): jnp.einsum('bij,bjk->bik', left_new.astype(jnp.bfloat16), basis_all, pref...  9.13 us
  transfers between devices with their start and end apart: 13, of which 12 were waited for; matrix products, arithmetic and copies ran while one was open for 14% of the time, Pallas kernels for 0%

profile of v1, /device:TPU:0, one launch (start us, length us, event | category | flops | bytes accessed | tf_op | source)
XLA Modules:
  0.0 441.0 jit_solution(7393316534938487174)
XLA Ops:
  8.0 33.7 %all-reduce.4.cloned.1.call-done = f32[2,1024,512]{2,1,0:T(8,128)} async-done(((f32[2,1024,512]{2,1,0:T(8,128)}), f32[2,1024,512]{2,1,0:T(8,128)}) %all-reduce.4.cloned.1.call-update) | async-done | bytes 4194320 | tf_op jit(solution)/shard_map/psum | solution.py:19
  42.5 175.1 %all-reduce.6.cloned.1.call-done = f32[2,1024,512]{2,1,0:T(8,128)} async-done(((f32[2,1024,512]{2,1,0:T(8,128)}), f32[2,1024,512]{2,1,0:T(8,128)}) %all-reduce.6.cloned.1.call-update) | async-done | bytes 4194320 | tf_op jit(solution)/shard_map/psum | solution.py:19
  220.4 11.4 %all-gather.14.cloned.1.call-done = bf16[2,1024,1024]{2,1,0:T(8,128)(2,1)} async-done(((bf16[2,512,1024]{2,1,0:T(8,128)(2,1)}), bf16[2,1024,1024]{2,1,0:T(8,128)(2,1)}) %all-gather.14.cloned.1.call-update) | async-done | bytes 4194320 | tf_op jit(solution)/shard_map/all_gather | solution.py:80
  231.8 9.1 %multiply_reduce_fusion = (f32[2]{0:T(128)S(1)}, f32[2,512,1024]{2,1,0:T(8,128)}) fusion(bf16[2,1024,1024]{2,1,0:T(8,128)(2,1)} %all-gather.14.cloned.1.call-done, f32[2,512,1024]{2,1,0:T(8,128)} %param.10, bf16[2,1024,512]{2,1,0:T(8,128)(2,1)S(1)} %multiply_convert_fusion.1, s32[]{:T(128)S(6)} %select_n.3), kind=kOutput, calls=%fused_computation.7 | convolution fusion | flops 3227516928 | bytes 15728652 | tf_op jit(solution)/shard_map/bij,bjk->bik/dot_general | solution.py:81
  243.4 4.1 multiply_convert_fusion
  247.7 14.9 %all-gather.16.cloned.1.call-done = bf16[2,1024,1024]{2,1,0:T(8,128)(2,1)} async-done(((bf16[2,512,1024]{2,1,0:T(8,128)(2,1)}), bf16[2,1024,1024]{2,1,0:T(8,128)(2,1)}) %all-gather.16.cloned.1.call-update) | async-done | bytes 4194320 | tf_op jit(solution)/shard_map/all_gather | solution.py:42
  262.6 6.5 %convolution_convert_fusion.2 = bf16[2,512,1024]{2,1,0:T(8,128)(2,1)} fusion(bf16[2,512,1024]{2,1,0:T(8,128)(2,1)} %multiply_convert_fusion, bf16[2,1024,1024]{2,1,0:T(8,128)(2,1)} %all-gather.16.cloned.1.call-done), kind=kOutput, calls=%fused_computation.19 | convolution fusion | flops 2148532224 | bytes 8388608 | tf_op jit(solution)/shard_map/bik,bjk->bij/dot_general | solution.py:44
  269.2 14.9 %all-gather.18.cloned.1.call-done = bf16[2,1024,1024]{2,1,0:T(8,128)(2,1)} async-done(((bf16[2,512,1024]{2,1,0:T(8,128)(2,1)}), bf16[2,1024,1024]{2,1,0:T(8,128)(2,1)}) %all-gather.18.cloned.1.call-update) | async-done | bytes 4194320 | tf_op jit(solution)/shard_map/all_gather | solution.py:48
  284.1 10.7 %add_convert_fusion.4 = bf16[2,512,1024]{2,1,0:T(8,128)(2,1)} fusion(bf16[2,512,1024]{2,1,0:T(8,128)(2,1)S(1)} %copy-done.1, bf16[2,1024,1024]{2,1,0:T(8,128)(2,1)} %all-gather.16.cloned.1.call-done, bf16[2,512,1024]{2,1,0:T(8,128)(2,1)} %convolution_convert_fusion.2, bf16[2,1024,1024]{2,1,0:T(8,128)(2,1)} %all-gather.18.cloned.1.call-done), kind=kOutput, calls=%fused_computation.4 | convolution fusion | flops 4304404480 | bytes 14680064 | tf_op jit(solution)/shard_map/bij,bjk->bik/dot_general | solution.py:56
  294.9 4.7 %convert_bitcast_fusion = bf16[2,1024,512]{2,1,0:T(8,128)(2,1)} fusion(bf16[2,512,1024]{2,1,0:T(8,128)(2,1)} %param.12, bf16[2,1024,512]{2,1,0:T(8,128)(2,1)} %copy-done.2, s32[]{:T(128)S(6)} %select_n.3), kind=kOutput, calls=%fused_computation.16 | convolution fusion | flops 1074790400 | bytes 5242884 | tf_op jit(solution)/shard_map/bji,bjk->bik/dot_general | solution.py:97
  299.8 10.0 %all-gather.20.cloned.1.call-done = bf16[2,1024,1024]{2,1,0:T(8,128)(2,1)} async-done(((bf16[2,512,1024]{2,1,0:T(8,128)(2,1)}), bf16[2,1024,1024]{2,1,0:T(8,128)(2,1)}) %all-gather.20.cloned.1.call-update) | async-done | bytes 4194320 | tf_op jit(solution)/shard_map/all_gather | solution.py:42
  309.9 5.9 %convolution_convert_fusion.1 = bf16[2,512,1024]{2,1,0:T(8,128)(2,1)} fusion(bf16[2,512,1024]{2,1,0:T(8,128)(2,1)S(1)} %copy-done.6, bf16[2,1024,1024]{2,1,0:T(8,128)(2,1)} %all-gather.20.cloned.1.call-done), kind=kOutput, calls=%fused_computation.18 | convolution fusion | flops 2148532224 | bytes 8388608 | tf_op jit(solution)/shard_map/bik,bjk->bij/dot_general | solution.py:44
  315.8 7.7 %reduce-scatter.2.cloned.1.call-done = bf16[2,512,512]{2,1,0:T(8,128)(2,1)} async-done(((bf16[2,1024,512]{2,1,0:T(8,128)(2,1)}), bf16[2,512,512]{2,1,0:T(8,128)(2,1)}) %reduce-scatter.2.cloned.1.call-update) | async-done | bytes 1048592 | tf_op jit(solution)/shard_map/reduce_scatter | solution.py:100
  323.5 6.2 %divide_convert_fusion = (bf16[2,512,512]{2,1,0:T(8,128)(2,1)S(1)}, f32[2,512,512]{2,1,0:T(8,128)}, f32[2,512,512]{2,1,0:T(8,128)}) fusion(f32[2,512,512]{2,1,0:T(8,128)} %param.15, f32[2,512,512]{2,1,0:T(8,128)} %param.14, bf16[2,512,512]{2,1,0:T(8,128)(2,1)} %reduce-scatter.2.cloned.1.call-done, bf16[512,512]{1,0:T(8,128)(2,1)S(1)} %copy-done), kind=kOutput, calls=%fused_computation.14 | convolution fusion | flops 542113792 | bytes 11010048 | tf_op jit(solution)/shard_map/dot_general | solution.py:104
  331.8 8.2 %all-gather.22.cloned.1.call-done = bf16[2,1024,1024]{2,1,0:T(8,128)(2,1)} async-done(((bf16[2,512,1024]{2,1,0:T(8,128)(2,1)}), bf16[2,1024,1024]{2,1,0:T(8,128)(2,1)}) %all-gather.22.cloned.1.call-update) | async-done | bytes 4194320 | tf_op jit(solution)/shard_map/all_gather | solution.py:48
  340.0 11.3 %add_convert_fusion.2 = bf16[2,512,1024]{2,1,0:T(8,128)(2,1)} fusion(bf16[2,512,1024]{2,1,0:T(8,128)(2,1)} %add_convert_fusion.4, bf16[2,1024,1024]{2,1,0:T(8,128)(2,1)} %all-gather.20.cloned.1.call-done, bf16[2,512,1024]{2,1,0:T(8,128)(2,1)} %convolution_convert_fusion.1, bf16[2,1024,1024]{2,1,0:T(8,128)(2,1)} %all-gather.22.cloned.1.call-done), kind=kOutput, calls=%fused_computation.2 | convolution fusion | flops 4304404480 | bytes 14680064 | tf_op jit(solution)/shard_map/bij,bjk->bik/dot_general | solution.py:56
  355.5 4.9 %fusion.1 = bf16[2,512,512]{1,2,0:T(8,128)(2,1)} fusion(bf16[2,512,512]{1,2,0:T(8,128)(2,1)} %copy.13, bf16[2,1024,512]{1,2,0:T(8,128)(2,1)} %all-gather.10.cloned.1.call-done, bf16[2,512,1024]{2,1,0:T(8,128)(2,1)} %param.12), kind=kOutput, calls=%fused_computation.13 | convolution fusion | flops 1075838976 | bytes 6291456 | tf_op jit(solution)/shard_map/bij,bjk->bik/dot_general | solution.py:117
  360.6 9.7 %all-gather.24.cloned.1.call-done = bf16[2,1024,1024]{2,1,0:T(8,128)(2,1)} async-done(((bf16[2,512,1024]{2,1,0:T(8,128)(2,1)}), bf16[2,1024,1024]{2,1,0:T(8,128)(2,1)}) %all-gather.24.cloned.1.call-update) | async-done | bytes 4194320 | tf_op jit(solution)/shard_map/all_gather | solution.py:42
  370.3 5.9 %convolution_convert_fusion = bf16[2,512,1024]{2,1,0:T(8,128)(2,1)} fusion(bf16[2,512,1024]{2,1,0:T(8,128)(2,1)S(1)} %copy-done.4, bf16[2,1024,1024]{2,1,0:T(8,128)(2,1)} %all-gather.24.cloned.1.call-done), kind=kOutput, calls=%fused_computation.17 | convolution fusion | flops 2148532224 | bytes 8388608 | tf_op jit(solution)/shard_map/bik,bjk->bij/dot_general | solution.py:44
  376.3 17.3 %all-reduce.8.cloned.1.call-done = f32[512,512]{1,0:T(8,128)} async-done(((f32[512,512]{1,0:T(8,128)}), f32[512,512]{1,0:T(8,128)}) %all-reduce.8.cloned.1.call-update) | async-done | bytes 1048592 | tf_op jit(solution)/shard_map/psum | solution.py:79
  403.8 3.5 all-gather.12.cloned.1.call-done
  407.3 3.9 copy.15
  411.3 12.5 %all-gather.26.cloned.1.call-done = bf16[2,1024,1024]{2,1,0:T(8,128)(2,1)} async-done(((bf16[2,512,1024]{2,1,0:T(8,128)(2,1)}), bf16[2,1024,1024]{2,1,0:T(8,128)(2,1)}) %all-gather.26.cloned.1.call-update) | async-done | bytes 4194320 | tf_op jit(solution)/shard_map/all_gather | solution.py:48
  423.8 10.7 %add_convert_fusion = bf16[2,512,1024]{2,1,0:T(8,128)(2,1)} fusion(bf16[2,512,1024]{2,1,0:T(8,128)(2,1)S(1)} %copy-done.5, bf16[2,1024,1024]{2,1,0:T(8,128)(2,1)} %all-gather.24.cloned.1.call-done, bf16[2,512,1024]{2,1,0:T(8,128)(2,1)} %convolution_convert_fusion, bf16[2,1024,1024]{2,1,0:T(8,128)(2,1)} %all-gather.26.cloned.1.call-done), kind=kOutput, calls=%fused_computation | convolution fusion | flops 4304404480 | bytes 14680064 | tf_op jit(solution)/shard_map/bij,bjk->bik/dot_general | solution.py:56
  (55 shorter events, 23.3 us)
Async XLA Ops:
  7.2 316.3 %copy-start = (bf16[512,512]{1,0:T(8,128)(2,1)S(1)}, bf16[512,512]{1,0:T(8,128)(2,1)}, u32[]{:S(2)}) copy-start(bf16[512,512]{1,0:T(8,128)(2,1)} %param.13) | copy-start | bytes 1572868
  7.2 34.5 %all-reduce.4.cloned.1.call-start = ((), (), s32[]{:S(2)}) async-start(), calls=%async_computation.1 | async-start | bytes 8388608 | tf_op jit(solution)/shard_map/psum | solution.py:19
  7.9 209.7 %all-reduce.6.cloned.1.call-start = ((), (), s32[]{:S(2)}) async-start(), calls=%async_computation.2 | async-start | bytes 8388608 | tf_op jit(solution)/shard_map/psum | solution.py:19
  41.7 190.1 %all-gather.14.cloned.1.call-start = ((), (), s32[]{:S(2)}) async-start(), calls=%async_computation.6 | async-start | bytes 6291456 | tf_op jit(solution)/shard_map/all_gather | solution.py:80
  42.4 220.2 %all-gather.16.cloned.1.call-start = ((), (), s32[]{:S(2)}) async-start(), calls=%async_computation.7 | async-start | bytes 6291456 | tf_op jit(solution)/shard_map/all_gather | solution.py:42
  220.4 20.6 %copy-start.2 = (bf16[2,1024,512]{2,1,0:T(8,128)(2,1)}, bf16[2,1024,512]{2,1,0:T(8,128)(2,1)S(1)}, u32[]{:S(2)}) copy-start(bf16[2,1024,512]{2,1,0:T(8,128)(2,1)S(1)} %multiply_convert_fusion.1) | copy-start | bytes 6291460
  247.6 36.5 %copy-start.1 = (bf16[2,512,1024]{2,1,0:T(8,128)(2,1)S(1)}, bf16[2,512,1024]{2,1,0:T(8,128)(2,1)}, u32[]{:S(2)}) copy-start(bf16[2,512,1024]{2,1,0:T(8,128)(2,1)} %multiply_convert_fusion) | copy-start | bytes 6291460
  247.6 36.5 %all-gather.18.cloned.1.call-start = ((), (), s32[]{:S(2)}) async-start(), calls=%async_computation.8 | async-start | bytes 6291456 | tf_op jit(solution)/shard_map/all_gather | solution.py:48
  269.1 40.7 %all-gather.20.cloned.1.call-start = ((), (), s32[]{:S(2)}) async-start(), calls=%async_computation.9 | async-start | bytes 6291456 | tf_op jit(solution)/shard_map/all_gather | solution.py:42
  294.8 15.0 %copy-start.6 = (bf16[2,512,1024]{2,1,0:T(8,128)(2,1)S(1)}, bf16[2,512,1024]{2,1,0:T(8,128)(2,1)}, u32[]{:S(2)}) copy-start(bf16[2,512,1024]{2,1,0:T(8,128)(2,1)} %add_convert_fusion.4) | copy-start | bytes 6291460
  294.9 28.6 %reduce-scatter.2.cloned.1.call-start = ((), (), s32[]{:S(2)}) async-start(), calls=%async_computation.3 | async-start | bytes 3145728 | tf_op jit(solution)/shard_map/reduce_scatter | solution.py:100
  299.6 40.4 %all-gather.22.cloned.1.call-start = ((), (), s32[]{:S(2)}) async-start(), calls=%async_computation.10 | async-start | bytes 6291456 | tf_op jit(solution)/shard_map/all_gather | solution.py:48
  315.7 39.7 %all-gather.10.cloned.1.call-start = ((), (), s32[]{:S(2)}) async-start(), calls=%async_computation.4 | async-start | bytes 3145728 | tf_op jit(solution)/shard_map/all_gather | solution.py:116
  331.7 19.6 %copy-start.3 = (bf16[2,1024,512]{2,1,0:T(8,128)(2,1)S(1)}, bf16[2,1024,512]{2,1,0:T(8,128)(2,1)}, u32[]{:S(2)}) copy-start(bf16[2,1024,512]{2,1,0:T(8,128)(2,1)} %copy-done.2) | copy-start | bytes 6291460
  331.7 38.6 %all-gather.24.cloned.1.call-start = ((), (), s32[]{:S(2)}) async-start(), calls=%async_computation.11 | async-start | bytes 6291456 | tf_op jit(solution)/shard_map/all_gather | solution.py:42
  351.3 42.3 %all-reduce.8.cloned.1.call-start = ((), (), s32[]{:S(2)}) async-start(), calls=%async_computation.13 | async-start | bytes 2097152 | tf_op jit(solution)/shard_map/psum | solution.py:79
  353.1 54.2 %all-gather.12.cloned.1.call-start = ((), (), s32[]{:S(2)}) async-start(), calls=%async_computation.5 | async-start | bytes 3145728 | tf_op jit(solution)/shard_map/all_gather | solution.py:119
  355.4 14.9 %copy-start.4 = (bf16[2,512,1024]{2,1,0:T(8,128)(2,1)S(1)}, bf16[2,512,1024]{2,1,0:T(8,128)(2,1)}, u32[]{:S(2)}) copy-start(bf16[2,512,1024]{2,1,0:T(8,128)(2,1)} %add_convert_fusion.2) | copy-start | bytes 6291460
  360.4 63.4 %all-gather.26.cloned.1.call-start = ((), (), s32[]{:S(2)}) async-start(), calls=%async_computation.12 | async-start | bytes 6291456 | tf_op jit(solution)/shard_map/all_gather | solution.py:48
  400.7 23.1 %copy-start.5 = (bf16[2,512,1024]{2,1,0:T(8,128)(2,1)S(1)}, bf16[2,512,1024]{2,1,0:T(8,128)(2,1)}, u32[]{:S(2)}) copy-start(bf16[2,512,1024]{2,1,0:T(8,128)(2,1)} %add_convert_fusion.2) | copy-start | bytes 6291460
Sparse Core Ops, SparseCore 0:
  10.5 31.1 all-reduce.3
  48.2 169.3 all-reduce.5
  219.2 12.6 all-gather.13
  247.7 14.8 all-gather.15
  269.2 14.8 all-gather.17
  295.0 14.8 all-gather.19
  312.7 10.7 reduce-scatter.1
  325.1 14.8 all-gather.21
  342.2 11.7 all-gather.9
  355.4 14.8 all-gather.23
  372.8 20.7 all-reduce.7
  395.5 11.7 all-gather.11
  408.9 14.8 all-gather.25
